TPU v7x, 32 devices: a whole 2x2x4 slice. The times are simulated.
32 devices in a mesh: section: 8 (over y, x, core), seq: 4 (over z).
Axes of the slice: x: 2, y: 2, z: 4, core: 2. Of those that a mesh axis runs over, the one named last changes fastest.
Arguments:
- grad_out: bfloat16 [8, 512, 2048], P('section', 'seq'), may hold values from -6 to 6
- block_input: bfloat16 [8, 512, 2048], P('section', 'seq'), may hold values from -5 to 5
- skip_saved: bfloat16 [8, 512, 2048], P('section', 'seq'), may hold values from -2 to 2
- saved_qkv: bfloat16 [8, 3, 512, 2048], P('section', None, None, 'seq'), may hold values from -16 to 16
- out_weight: bfloat16 [8, 2048, 2048], P('section', 'seq'), may hold values from -0.125 to 0.125
- qkv_weight: bfloat16 [8, 3, 2048, 2048], P('section', None, 'seq'), may hold values from -0.125 to 0.125
- gate: float32 [8, 2048], P('section'), may hold values from 0.5 to 1.5
- norm_scale: float32 [8, 2048], P('section'), may hold values from -0.5 to 0.5
- skip_gain: float32 [8, 2048], P('section'), may hold values from 0.3 to 1.5
Outputs:
- next_grad: bfloat16 [8, 512, 2048], P('section', 'seq')
- down_grad: bfloat16 [8, 512, 2048], P('section', 'seq')
- gain_grad: float32 [8, 2048], P('section')
All inputs are finite; a program needn't handle non-finite values.
Results may differ from a plain program's by a relative error of at most 0.015.
Values may be sent and summed in bfloat16 or wider, within the bound.
No kernel may reach another device: no remote copies, remote signals or barrier semaphores. Data moves between devices by JAX's collectives and lax.ppermute only.
A program may use at most 128 MiB of HBM per device.

v0:
```python
import jax
import jax.numpy as jnp
from jax import lax
from jax.sharding import PartitionSpec as P

HEAD_DIM = 128
norm_eps = 1e-06


def passed_along(block, axis, distance):
    devices = range(lax.axis_size(axis))
    route = [(i - distance, i) for i in devices if i - distance in devices]
    return lax.ppermute(block, axis, route)


def local_attention(query_all, keys_all, values_all, grad_cols, head_count, head_size):
    factor = head_size ** (-0.5)
    total_rows = query_all.shape[0]
    block_rows = min(512, total_rows)
    block_count = total_rows // block_rows
    query_out, keys_out, values_out = ([], [], [])
    for head_idx in range(head_count):
        lower = head_idx * head_size
        query_head = query_all[:, lower : lower + head_size]
        keys_head = keys_all[:, lower : lower + head_size]
        values_head = values_all[:, lower : lower + head_size]
        grad_head = grad_cols[lower : lower + head_size, :]
        query_blocks = query_head.reshape(block_count, block_rows, head_size)
        grad_blocks = jnp.moveaxis(grad_head.reshape(head_size, block_count, block_rows), 1, 0)

        def visit(carried, blocks):
            keys_acc, values_acc = carried
            query_blk, grad_blk = blocks
            scores = (
                jnp.einsum("qd,kd->qk", query_blk, keys_head, preferred_element_type=jnp.float32)
                * factor
            )
            scores = scores - jnp.max(scores, axis=-1, keepdims=True)
            weights = jnp.exp(scores)
            probs = weights / jnp.sum(weights, axis=-1, keepdims=True)
            dprobs = jnp.einsum(
                "dq,kd->qk", grad_blk, values_head, preferred_element_type=jnp.float32
            )
            delta = jnp.sum(probs * dprobs, axis=-1, keepdims=True)
            dscores = probs * (dprobs - delta)
            probs_low = probs.astype(jnp.bfloat16)
            dscores_low = dscores.astype(jnp.bfloat16)
            values_acc = values_acc + jnp.einsum(
                "qk,dq->kd", probs_low, grad_blk, preferred_element_type=jnp.float32
            )
            keys_acc = keys_acc + jnp.einsum(
                "qk,qd->kd", dscores_low, query_blk, preferred_element_type=jnp.float32
            )
            query_grad = (
                jnp.einsum("qk,kd->qd", dscores_low, keys_head, preferred_element_type=jnp.float32)
                * factor
            ).astype(jnp.bfloat16)
            return ((keys_acc, values_acc), query_grad)

        empty = jnp.zeros((total_rows, head_size), jnp.float32)
        (keys_acc, values_acc), query_grads = lax.scan(
            visit, (empty, empty), (query_blocks, grad_blocks)
        )
        query_out.append(query_grads.reshape(total_rows, head_size))
        keys_out.append((keys_acc * factor).astype(jnp.bfloat16))
        values_out.append(values_acc.astype(jnp.bfloat16))
    return (
        jnp.concatenate(query_out, axis=1),
        jnp.concatenate(keys_out, axis=1),
        jnp.concatenate(values_out, axis=1),
    )


def on_device(
    grad_out,
    block_input,
    skip_saved,
    saved_qkv,
    out_weight,
    qkv_weight,
    gate,
    norm_scale,
    skip_gain,
):
    seq_count = lax.axis_size("seq")
    incoming_gradient = grad_out[0]
    tok_rows, features = incoming_gradient.shape
    local_width = out_weight.shape[1]
    head_size = HEAD_DIM
    head_count = local_width // head_size
    feat_group = features // seq_count
    gated = (incoming_gradient.astype(jnp.float32) * gate[0]).astype(jnp.bfloat16)
    weight_out = out_weight[0]
    rows_in = lax.all_gather(gated, "seq", axis=0, tiled=True)
    row_count = rows_in.shape[0]
    terms = jnp.einsum(
        "rgs,hgs->ghr",
        rows_in.reshape(row_count, seq_count, feat_group),
        weight_out.reshape(local_width, seq_count, feat_group),
        preferred_element_type=jnp.float32,
    )
    rounded = lax.optimization_barrier(terms.astype(jnp.bfloat16))
    grad_cols = jnp.sum(rounded.astype(jnp.float32), axis=0).astype(jnp.bfloat16)
    query_grad, keys_grad, values_grad = local_attention(
        saved_qkv[0, 0], saved_qkv[0, 1], saved_qkv[0, 2], grad_cols, head_count, head_size
    )
    weight_qkv = qkv_weight[0]
    total = jnp.dot(query_grad, weight_qkv[0], preferred_element_type=jnp.float32)
    total = total + jnp.dot(keys_grad, weight_qkv[1], preferred_element_type=jnp.float32)
    total = total + jnp.dot(values_grad, weight_qkv[2], preferred_element_type=jnp.float32)
    normed_grad = lax.psum_scatter(
        total.astype(jnp.bfloat16), "seq", scatter_dimension=0, tiled=True
    ).astype(jnp.float32)
    xvalue = block_input[0].astype(jnp.float32)
    mean_x = jnp.mean(xvalue, axis=-1, keepdims=True)
    centered_input = xvalue - mean_x
    var_x = jnp.mean(centered_input * centered_input, axis=-1, keepdims=True)
    inverse_deviation = 1.0 / jnp.sqrt(var_x + norm_eps)
    normalized_input = centered_input * inverse_deviation
    scaled_gradient = normed_grad * (1.0 + norm_scale[0])
    input_gradient = incoming_gradient.astype(jnp.float32) + inverse_deviation * (
        scaled_gradient
        - jnp.mean(scaled_gradient, axis=-1, keepdims=True)
        - normalized_input * jnp.mean(scaled_gradient * normalized_input, axis=-1, keepdims=True)
    )
    hand_grad = input_gradient.astype(jnp.bfloat16)
    next_grad = passed_along(hand_grad, "section", 1)
    last_flag = jnp.where(
        lax.axis_index("section") == lax.axis_size("section") - 1, 1.0, 0.0
    ).astype(jnp.float32)
    down_grad = ((skip_gain[0] + last_flag) * input_gradient).astype(jnp.bfloat16)
    gain_local = jnp.sum(input_gradient * skip_saved[0].astype(jnp.float32), axis=0)
    gain_grad = lax.psum(gain_local, "seq")
    return (next_grad[None], down_grad[None], gain_grad[None])


def solution(mesh):
    placed = (
        P("section", "seq", None),
        P("section", "seq", None),
        P("section", "seq", None),
        P("section", None, None, "seq"),
        P("section", "seq", None),
        P("section", None, "seq", None),
        P("section", None),
        P("section", None),
        P("section", None),
    )
    return jax.shard_map(
        on_device,
        mesh=mesh,
        in_specs=placed,
        out_specs=(P("section", "seq", None), P("section", "seq", None), P("section", None)),
        check_vma=False,
    )
```

profile of v0, /device:TPU:0, one launch (start us, length us, event | category | flops | bytes accessed | tf_op | source)
XLA Modules:
  0.0 152.5 jit_solution(16319385925375333558)
XLA Ops:
  7.2 1.9 %fusion.29 = bf16[128,2048]{1,0:T(8,128)(2,1)} fusion(bf16[1,128,2048]{2,1,0:T(8,128)(2,1)} %param.9, f32[2048]{0:T(1024)} %bitcast.73), kind=kLoop, calls=%fused_computation.49 | loop fusion | flops 786432 | bytes 1056768 | tf_op jit(solution)/shard_map/convert_element_type | solution.py:92
  9.2 4.6 %reshape_squeeze.3 = bf16[512,4,512]{2,1,0:T(4,128)(2,1)} reshape(bf16[1,512,2048]{2,1,0:T(8,128)(2,1)} %param.13) | data formatting | bytes 4194304 | tf_op jit(solution)/shard_map/reshape;squeeze | solution.py:99
  13.8 0.9 slice_bitcast_fusion.2
  15.3 0.3 fusion.106
  15.8 0.3 fusion.107
  16.3 0.3 fusion.108
  16.8 41.7 %all-gather.2.cloned.1.call-done = bf16[512,2048]{1,0:T(8,128)(2,1)} async-done(((bf16[128,2048]{1,0:T(8,128)(2,1)}), bf16[512,2048]{1,0:T(8,128)(2,1)}) %all-gather.2.cloned.1.call-update) | async-done | bytes 2097168 | tf_op jit(solution)/shard_map/all_gather | solution.py:94
  58.5 3.9 %copy.16 = bf16[512,2048]{0,1:T(8,128)(2,1)} copy(bf16[512,2048]{1,0:T(8,128)(2,1)} %all-gather.2.cloned.1.call-done) | data formatting | bytes 4194304 | tf_op jit(solution)/shard_map/all_gather | solution.py:94
  62.5 5.1 %convert_bitcast_fusion = bf16[4,512,512]{1,2,0:T(8,128)(2,1)} fusion(bf16[512,4,512]{0,2,1:T(8,128)(2,1)} %bitcast.65, bf16[512,4,512]{2,1,0:T(4,128)(2,1)} %reshape_squeeze.3), kind=kOutput, calls=%fused_computation.11 | convolution fusion | flops 1074790400 | bytes 6291456 | tf_op jit(solution)/shard_map/rgs,hgs->ghr/dot_general | solution.py:96
  67.6 2.9 %reduce_sum.140 = bf16[512,512]{0,1:T(8,128)(2,1)} reduce(bf16[4,512,512]{1,2,0:T(8,128)(2,1)} %convert_bitcast_fusion, bf16[]{:T(256)} %constant.84.clone.1), dimensions={0}, to_apply=%region_4.5 | reduce | flops 786432 | bytes 2621442 | tf_op jit(solution)/shard_map/reduce_sum | solution.py:103
  70.4 1.7 %convolution_convert_fusion = bf16[512,128]{0,1:T(8,128)(2,1)S(1)} fusion(bf16[512,512]{0,1:T(8,128)(2,1)} %reduce_sum.140, f32[512,512]{0,1:T(8,128)} %copy-done, f32[512]{0:T(512)S(1)} %fusion.39, f32[512]{0:T(512)S(1)} %get-tuple-element.84), kind=kOutput, calls=%fused_computation.36 | convolution fusion | flops 67960832 | bytes 1314816 | tf_op jit(solution)/shard_map/while/body/eval_jaxpr/qk,dq->kd/dot_general | solution.py:48
  72.3 0.3 multiply_reduce_fusion
  72.9 0.7 copy-done.4
  74.3 0.4 convolution_convert_fusion.1
  74.6 0.3 multiply_reduce_fusion.1
  75.8 0.4 convolution_convert_fusion.2
  76.2 0.3 multiply_reduce_fusion.2
  76.5 0.4 convolution_convert_fusion.3
  76.9 0.3 multiply_reduce_fusion.3
  77.5 0.3 fusion.17
  79.1 0.8 slice-done.1
  79.9 1.3 fusion.3
  81.2 1.3 fusion.1
  82.5 2.8 %add_convert_fusion = bf16[512,2048]{1,0:T(8,128)(2,1)} fusion(f32[512,2048]{1,0:T(8,128)S(1)} %fusion.3, f32[512,2048]{1,0:T(8,128)S(1)} %fusion.1, bf16[1,3,512,2048]{3,2,1,0:T(8,128)(2,1)S(1)} %bitcast.67, bf16[512,128]{0,1:T(8,128)(2,1)S(1)} %convolution_convert_fusion, bf16[512,128]{0,1:T(8,128)(2,1)S(1)} %convolution_convert_fusion.1, ...), kind=kOutput, calls=%fused_computation | convolution fusion | flops 1078984704 | bytes 13107200 | tf_op jit(solution)/shard_map/dot_general | solution.py:110
  85.3 1.0 copy-done.2
  86.8 41.1 %reduce-scatter.2.cloned.1.call-done = bf16[128,2048]{1,0:T(8,128)(2,1)} async-done(((bf16[512,2048]{1,0:T(8,128)(2,1)}), bf16[128,2048]{1,0:T(8,128)(2,1)}) %reduce-scatter.2.cloned.1.call-update) | async-done | bytes 524304 | tf_op jit(solution)/shard_map/reduce_scatter | solution.py:111
  127.9 1.4 fusion.31
  129.3 1.8 %fusion.30 = (f32[2048]{0:T(1024)S(1)}, f32[128,2048]{1,0:T(8,128)S(1)}) fusion(bf16[1,128,2048]{2,1,0:T(8,128)(2,1)S(1)} %copy-done.9, f32[128]{0:T(128)S(1)} %get-tuple-element.116, f32[128]{0:T(128)S(1)} %broadcast_multiply_fusion.2, bf16[1,128,2048]{2,1,0:T(8,128)(2,1)S(1)} %copy-done.2, f32[128]{0:T(128)S(1)} %get-tuple-element.117, ...), kind=kLoop, calls=%fused_computation.51 | loop fusion | flops 3667968 | bytes 3164160 | tf_op jit(solution)/shard_map/reduce_sum | solution.py:132
  131.2 0.9 fusion.40
  132.1 1.4 collective-permute-start
  133.5 11.4 %psum.7 = f32[1,2048]{1,0:T(1,128)} all-reduce(f32[1,2048]{1,0:T(1,128)S(1)} %bitcast.72), channel_id=1, replica_groups=mesh['section'=8,'seq'=4] {'seq'}, use_global_device_ids=true, to_apply=%region_19.20 | all-reduce | flops 2048 | bytes 16384 | tf_op jit(solution)/shard_map/psum | solution.py:133
  144.9 0.8 copy.25
  (58 shorter events, 5.1 us)
Async XLA Ops:
  7.2 51.4 %all-gather.2.cloned.1.call-start = ((), (), s32[]{:S(2)}) async-start(), calls=%async_computation.1 | async-start | bytes 2621440 | tf_op jit(solution)/shard_map/all_gather | solution.py:94
  9.2 4.7 %copy-start.8 = (bf16[1,3,512,512]{3,2,1,0:T(8,128)(2,1)S(1)}, bf16[1,3,512,512]{3,2,1,0:T(8,128)(2,1)}, u32[]{:S(2)}) copy-start(bf16[1,3,512,512]{3,2,1,0:T(8,128)(2,1)} %param.12) | copy-start | bytes 4718596
  9.2 118.7 %reduce-scatter.2.cloned.1.call-start = ((), (), s32[]{:S(2)}) async-start(), calls=%async_computation.2 | async-start | bytes 2621440 | tf_op jit(solution)/shard_map/reduce_scatter | solution.py:111
  14.7 1.6 %copy-start.3 = (bf16[512,512]{1,0:T(8,128)(2,1)}, bf16[512,512]{1,0:T(8,128)(2,1)S(1)}, u32[]{:S(2)}) copy-start(bf16[512,512]{1,0:T(8,128)(2,1)S(1)} %get-tuple-element.71) | copy-start | bytes 1572868
  14.7 1.6 %copy-start.5 = (bf16[512,512]{1,0:T(8,128)(2,1)}, bf16[512,512]{1,0:T(8,128)(2,1)S(1)}, u32[]{:S(2)}) copy-start(bf16[512,512]{1,0:T(8,128)(2,1)S(1)} %get-tuple-element.81) | copy-start | bytes 1572868
  15.1 1.0 copy-start
  70.4 1.7 %copy-start.1 = (f32[512,512]{0,1:T(8,128)S(1)}, f32[512,512]{0,1:T(8,128)}, u32[]{:S(2)}) copy-start(f32[512,512]{0,1:T(8,128)} %copy-done) | copy-start | bytes 3145732
  70.4 1.7 %copy-start.10 = (bf16[512,512]{1,0:T(8,128)(2,1)S(1)}, bf16[512,512]{1,0:T(8,128)(2,1)}, u32[]{:S(2)}) copy-start(bf16[512,512]{1,0:T(8,128)(2,1)} %get-tuple-element.80) | copy-start | bytes 1572868
  70.4 1.9 %copy-start.11 = (bf16[512,512]{0,1:T(8,128)(2,1)S(1)}, bf16[512,512]{0,1:T(8,128)(2,1)}, u32[]{:S(2)}) copy-start(bf16[512,512]{0,1:T(8,128)(2,1)} %reduce_sum.140) | copy-start | bytes 1572868
  72.6 1.0 copy-start.4
  72.6 1.4 copy-start.6
  76.9 2.2 %slice-start = ((s8[6291456]{0:T(1024)(128)(4,1)}), s8[4194304]{0:T(1024)(128)(4,1)S(1)}, s32[]{:S(2)}) async-start(s8[6291456]{0:T(1024)(128)(4,1)} %bitcast.66), calls=%async_computation.3 | async-start | bytes 8388608
  77.2 2.6 %slice-start.1 = ((s8[6291456]{0:T(1024)(128)(4,1)}), s8[2097152]{0:T(1024)(128)(4,1)S(1)}, s32[]{:S(2)}) async-start(s8[6291456]{0:T(1024)(128)(4,1)} %bitcast.66), calls=%async_computation.4 | async-start | bytes 4194304
  85.3 1.0 copy-start.2
  85.3 1.5 copy-start.12
  85.3 1.5 %copy-start.13 = (f32[1,2048]{1,0:T(1,128)S(1)}, f32[1,2048]{1,0:T(1,128)}, u32[]{:S(2)}) copy-start(f32[1,2048]{1,0:T(1,128)} %param.17) | copy-start | bytes 24580
  85.3 44.0 %copy-start.7 = (bf16[1,128,2048]{2,1,0:T(8,128)(2,1)S(1)}, bf16[1,128,2048]{2,1,0:T(8,128)(2,1)}, u32[]{:S(2)}) copy-start(bf16[1,128,2048]{2,1,0:T(8,128)(2,1)} %param.9) | copy-start | bytes 1572868
  85.3 44.0 %copy-start.9 = (bf16[1,128,2048]{2,1,0:T(8,128)(2,1)S(1)}, bf16[1,128,2048]{2,1,0:T(8,128)(2,1)}, u32[]{:S(2)}) copy-start(bf16[1,128,2048]{2,1,0:T(8,128)(2,1)} %param.11) | copy-start | bytes 1572868
  132.1 12.8 %collective-permute-start = (bf16[128,2048]{1,0:T(8,128)(2,1)S(1)}, bf16[128,2048]{1,0:T(8,128)(2,1)S(1)}, u32[]{:S(2)}, u32[]{:S(2)}) collective-permute-start(bf16[128,2048]{1,0:T(8,128)(2,1)S(1)} %get-tuple-element.83), channel_id=1, source_target_pairs={{0,4},{4,8},{8,12},{12,16},{16,20},{20,24},{24,28},{1,5},{5,9},{9,... | collective-permute-start | bytes 1572872 | tf_op jit(solution)/shard_map/ppermute | solution.py:13
Sparse Core Ops, SparseCore 0:
  10.1 48.3 all-gather.1
  85.4 42.4 reduce-scatter.1
where the time goes:
time: 153 us
  waiting for transfers between devices  82.8 us (54%)
  matrix products  18.2 us (12%)
  between operations  14.3 us (9%)
  local copies, waits for them, and re-layouts  13 us (8%)
  other arithmetic  11.4 us (7%)
  blocking collectives  11.4 us (7%)
    all_gather x1, waiting for transfers between devices, on_device(): rows_in = lax.all_gather(gated, 'seq', axis=0, tiled=True)  41.7 us
    reduce_scatter x1, waiting for transfers between devices, on_device(): lax.psum_scatter(total.astype(jnp.bfloat16), 'seq', scatter_dimension=0,...  41.1 us
    psum x1, blocking collectives, on_device(): gain_grad = lax.psum(gain_local, 'seq')  11.4 us
    dot_general x1, matrix products, on_device(): jnp.einsum('rgs,hgs->ghr', rows_in.reshape(row_count, seq_count, feat_gro...  5.12 us
    another operation x1, local copies, waits for them, and re-layouts, on_device(): weight_out.reshape(local_width, seq_count, feat_group)  4.61 us
    all_gather x1, local copies, waits for them, and re-layouts, on_device(): rows_in = lax.all_gather(gated, 'seq', axis=0, tiled=True)  3.93 us
    unnamed x33, local copies, waits for them, and re-layouts  3.57 us
  transfers between devices with their start and end apart: 3, of which 2 were waited for; matrix products, arithmetic and copies ran while one was open for 5% of the time, Pallas kernels for 0%

commit v1 on v0

--- a/solution.py
+++ b/solution.py
@@ -5,6 +5,23 @@
 
 HEAD_DIM = 128
 norm_eps = 1e-06
+
+
+def laid_out(blocks, dim):
+    blocks = jnp.moveaxis(blocks, 0, dim)
+    dims = blocks.shape
+    return blocks.reshape(*dims[:dim], dims[dim] * dims[dim + 1], *dims[dim + 2 :])
+
+
+def gather_around(value, axis, dim):
+    size = lax.axis_size(axis)
+    forward = [(i, (i + 1) % size) for i in range(size)]
+    blocks = [value]
+    while len(blocks) < size:
+        blocks.append(lax.ppermute(blocks[-1], axis, forward))
+    index = lax.axis_index(axis)
+    blocks = jnp.stack(blocks)[(index - jnp.arange(size)) % size]
+    return laid_out(blocks, dim)
 
 
 def passed_along(block, axis, distance):
@@ -91,7 +108,7 @@
     feat_group = features // seq_count
     gated = (incoming_gradient.astype(jnp.float32) * gate[0]).astype(jnp.bfloat16)
     weight_out = out_weight[0]
-    rows_in = lax.all_gather(gated, "seq", axis=0, tiled=True)
+    rows_in = gather_around(gated, "seq", 0)
     row_count = rows_in.shape[0]
     terms = jnp.einsum(
         "rgs,hgs->ghr",

time: 153 us -> 156 us (1.020)
  waiting for transfers between devices: 82.8 us -> 72.4 us
  local copies, waits for them, and re-layouts: 13 us -> 18.8 us
  other arithmetic: 11.4 us -> 15.4 us
  starting transfers between devices: 1.45 us -> 4.47 us
    all_gather x1 -> x0, waiting for transfers between devices: 41.7 us -> none  [on_device(): rows_in = lax.all_gather(gated, 'seq', axis=0, tiled=True)]
    ppermute x0 -> x3, waiting for transfers between devices: none -> 32.3 us  [gather_around(): blocks.append(lax.ppermute(blocks[-1], axis, forward))]
    another operation x0 -> x1, local copies, waits for them, and re-layouts: none -> 4.51 us  [on_device(): rows_in.reshape(row_count, seq_count, feat_group)]
    all_gather x1 -> x0, local copies, waits for them, and re-layouts: 3.93 us -> none  [on_device(): rows_in = lax.all_gather(gated, 'seq', axis=0, tiled=True)]
    gather x0 -> x1, local copies, waits for them, and re-layouts: none -> 3.6 us  [gather_around(): blocks = jnp.stack(blocks)[(index - jnp.arange(size)) % size]]
    ppermute x0 -> x3, starting transfers between devices: none -> 3.06 us  [gather_around(): blocks.append(lax.ppermute(blocks[-1], axis, forward))]
    another operation x0 -> x1, other arithmetic: none -> 2.91 us  [gather_around(): blocks = jnp.stack(blocks)[(index - jnp.arange(size)) % size]]
  transfers between devices with their start and end apart: 3 -> 5, of which waited for: 2 -> 4; matrix products, arithmetic and copies ran while one was open for 5% -> 7% of each run, Pallas kernels for 0% -> 0%
where the time goes in v1:
time: 156 us
  waiting for transfers between devices  72.4 us (46%)
  matrix products  18.9 us (12%)
  local copies, waits for them, and re-layouts  18.8 us (12%)
  other arithmetic  15.4 us (10%)
  between operations  14.3 us (9%)
  blocking collectives  11.4 us (7%)
  starting transfers between devices  4.47 us (3%)
    reduce_scatter x1, waiting for transfers between devices, on_device(): lax.psum_scatter(total.astype(jnp.bfloat16), 'seq', scatter_dimension=0,...  40 us
    ppermute x3, waiting for transfers between devices, gather_around(): blocks.append(lax.ppermute(blocks[-1], axis, forward))  32.3 us
    psum x1, blocking collectives, on_device(): gain_grad = lax.psum(gain_local, 'seq')  11.4 us
    dot_general x1, matrix products, on_device(): jnp.einsum('rgs,hgs->ghr', rows_in.reshape(row_count, seq_count, feat_gro...  5 us
    another operation x1, local copies, waits for them, and re-layouts, on_device(): rows_in.reshape(row_count, seq_count, feat_group)  4.51 us
    another operation x1, local copies, waits for them, and re-layouts, on_device(): weight_out.reshape(local_width, seq_count, feat_group)  4.5 us
    unnamed x33, local copies, waits for them, and re-layouts  3.93 us
    gather x1, local copies, waits for them, and re-layouts, gather_around(): blocks = jnp.stack(blocks)[(index - jnp.arange(size)) % size]  3.6 us
  transfers between devices with their start and end apart: 5, of which 4 were waited for; matrix products, arithmetic and copies ran while one was open for 7% of the time, Pallas kernels for 0%

profile of v1, /device:TPU:0, one launch (start us, length us, event | category | flops | bytes accessed | tf_op | source)
XLA Modules:
  0.0 155.7 jit_solution(4805847330519669015)
XLA Ops:
  7.2 1.9 %fusion.34 = bf16[128,2048]{1,0:T(8,128)(2,1)} fusion(bf16[1,128,2048]{2,1,0:T(8,128)(2,1)} %param.9, f32[2048]{0:T(1024)} %bitcast.77), kind=kLoop, calls=%fused_computation.54 | loop fusion | flops 786432 | bytes 1056768 | tf_op jit(solution)/shard_map/convert_element_type | solution.py:109
  9.2 3.1 %collective-permute-start = (bf16[128,2048]{1,0:T(8,128)(2,1)}, bf16[128,2048]{1,0:T(8,128)(2,1)}, u32[]{:S(2)}, u32[]{:S(2)}) collective-permute-start(bf16[128,2048]{1,0:T(8,128)(2,1)} %fusion.34), channel_id=1, source_target_pairs={{0,1},{1,2},{2,3},{3,0},{4,5},{5,6},{6,7},{7,4},{8,9},{9,10},{10,1... | collective-permute-start | bytes 1572872 | tf_op jit(solution)/shard_map/ppermute | solution.py:21
  12.2 2.3 %slice_bitcast_fusion.2 = (bf16[512,512]{1,0:T(8,128)(2,1)S(1)}, bf16[512,512]{1,0:T(8,128)(2,1)}, bf16[512,512]{1,0:T(8,128)(2,1)S(1)}) fusion(bf16[1,3,512,512]{3,2,1,0:T(8,128)(2,1)} %param.12), kind=kLoop, calls=%fused_computation.109 | loop fusion | bytes 3145728 | tf_op jit(solution)/shard_map/squeeze | solution.py:122
  15.3 0.5 copy-done
  16.5 9.9 %collective-permute-done = bf16[128,2048]{1,0:T(8,128)(2,1)} collective-permute-done((bf16[128,2048]{1,0:T(8,128)(2,1)}, bf16[128,2048]{1,0:T(8,128)(2,1)}, u32[]{:S(2)}, u32[]{:S(2)}) %collective-permute-start) | collective-permute-done | bytes 524320 | tf_op jit(solution)/shard_map/ppermute | solution.py:21
  26.5 1.3 fusion.117
  28.0 13.7 %collective-permute-done.1 = bf16[128,2048]{1,0:T(8,128)(2,1)} collective-permute-done((bf16[128,2048]{1,0:T(8,128)(2,1)}, bf16[128,2048]{1,0:T(8,128)(2,1)}, u32[]{:S(2)}, u32[]{:S(2)}) %collective-permute-start.1) | collective-permute-done | bytes 524320 | tf_op jit(solution)/shard_map/ppermute | solution.py:21
  41.7 4.5 %reshape_squeeze.3 = bf16[512,4,512]{2,1,0:T(4,128)(2,1)} reshape(bf16[1,512,2048]{2,1,0:T(8,128)(2,1)} %param.13) | data formatting | bytes 4194304 | tf_op jit(solution)/shard_map/reshape;squeeze | solution.py:116
  46.2 1.1 fusion.35
  47.3 8.7 %collective-permute-done.2 = bf16[128,2048]{1,0:T(8,128)(2,1)} collective-permute-done((bf16[128,2048]{1,0:T(8,128)(2,1)}, bf16[128,2048]{1,0:T(8,128)(2,1)}, u32[]{:S(2)}, u32[]{:S(2)}) %collective-permute-start.2) | collective-permute-done | bytes 524320 | tf_op jit(solution)/shard_map/ppermute | solution.py:21
  56.0 2.9 %pad_maximum_fusion = bf16[4,128,2048]{2,1,0:T(8,128)(2,1)} fusion(bf16[1,128,2048]{2,1,0:T(8,128)(2,1)} %bitcast.7, bf16[1,128,2048]{2,1,0:T(8,128)(2,1)} %bitcast.6, bf16[1,128,2048]{2,1,0:T(8,128)(2,1)} %bitcast.5, bf16[1,128,2048]{2,1,0:T(8,128)(2,1)S(1)} %fusion.35), kind=kLoop, calls=%fused_computation.2 | loop fusion | flops 3145728 | bytes 4194304 | tf_op jit(solution)/shard_map/stack | solution.py:23
  58.9 3.6 %gather_fusion = bf16[4,128,2048]{2,1,0:T(8,128)(2,1)} fusion(bf16[4,128,2048]{2,1,0:T(8,128)(2,1)} %pad_maximum_fusion, s32[1024]{0:T(1024)S(1)} %pad_clamp_fusion), kind=kCustom, calls=%fused_computation | custom fusion | bytes 4194320 | tf_op jit(solution)/shard_map/gather | solution.py:23
  62.5 4.5 %reshape_reshape.3 = bf16[512,4,512]{2,1,0:T(4,128)(2,1)} reshape(bf16[4,128,2048]{2,1,0:T(8,128)(2,1)} %gather_fusion) | data formatting | bytes 4194304 | tf_op jit(solution)/shard_map/reshape;reshape | solution.py:115
  67.0 5.0 %convert_bitcast_fusion = bf16[4,512,512]{1,2,0:T(8,128)(2,1)} fusion(bf16[512,4,512]{2,1,0:T(4,128)(2,1)} %reshape_squeeze.3, bf16[512,4,512]{2,1,0:T(4,128)(2,1)} %reshape_reshape.3), kind=kOutput, calls=%fused_computation.14 | convolution fusion | flops 1074790400 | bytes 6291456 | tf_op jit(solution)/shard_map/rgs,hgs->ghr/dot_general | solution.py:113
  72.0 2.9 %reduce_sum.140 = bf16[512,512]{0,1:T(8,128)(2,1)} reduce(bf16[4,512,512]{1,2,0:T(8,128)(2,1)} %convert_bitcast_fusion, bf16[]{:T(256)} %constant.104.clone.1), dimensions={0}, to_apply=%region_4.5 | reduce | flops 786432 | bytes 2621442 | tf_op jit(solution)/shard_map/reduce_sum | solution.py:120
  74.9 1.7 %convolution_convert_fusion = bf16[512,128]{1,0:T(8,128)(2,1)S(1)} fusion(bf16[512,512]{0,1:T(8,128)(2,1)} %reduce_sum.140, f32[512,512]{0,1:T(8,128)} %copy-done, f32[512]{0:T(512)S(1)} %fusion.45, f32[512]{0:T(512)S(1)} %get-tuple-element.84), kind=kOutput, calls=%fused_computation.41 | convolution fusion | flops 67960832 | bytes 1314816 | tf_op jit(solution)/shard_map/while/body/eval_jaxpr/qk,dq->kd/dot_general | solution.py:65
  77.4 0.7 copy-done.7
  78.4 0.3 fusion.20
  82.3 0.3 fusion.18
  83.3 0.3 fusion.17
  83.6 0.7 slice-done.1
  84.3 1.3 fusion.3
  85.6 1.3 fusion.1
  86.9 2.6 %add_convert_fusion = bf16[512,2048]{1,0:T(8,128)(2,1)} fusion(f32[512,2048]{1,0:T(8,128)S(1)} %fusion.3, f32[512,2048]{1,0:T(8,128)S(1)} %fusion.1, bf16[1,3,512,2048]{3,2,1,0:T(8,128)(2,1)S(1)} %bitcast.73, bf16[512,128]{1,0:T(8,128)(2,1)S(1)} %convolution_convert_fusion, bf16[512,128]{1,0:T(8,128)(2,1)S(1)} %convolution_convert_fusion.1, ...), kind=kOutput, calls=%fused_computation.1 | convolution fusion | flops 1078984704 | bytes 13107200 | tf_op jit(solution)/shard_map/dot_general | solution.py:127
  89.6 1.0 copy-done.2
  91.1 40.0 %reduce-scatter.2.cloned.1.call-done = bf16[128,2048]{1,0:T(8,128)(2,1)} async-done(((bf16[512,2048]{1,0:T(8,128)(2,1)}), bf16[128,2048]{1,0:T(8,128)(2,1)}) %reduce-scatter.2.cloned.1.call-update) | async-done | bytes 524304 | tf_op jit(solution)/shard_map/reduce_scatter | solution.py:128
  131.1 1.4 fusion.37
  132.5 1.8 %fusion.36 = (f32[2048]{0:T(1024)S(1)}, f32[128,2048]{1,0:T(8,128)S(1)}) fusion(bf16[1,128,2048]{2,1,0:T(8,128)(2,1)S(1)} %copy-done.8, f32[128]{0:T(128)S(1)} %get-tuple-element.116, f32[128]{0:T(128)S(1)} %broadcast_multiply_fusion.2, bf16[1,128,2048]{2,1,0:T(8,128)(2,1)S(1)} %copy-done.2, f32[128]{0:T(128)S(1)} %get-tuple-element.117, ...), kind=kLoop, calls=%fused_computation.57 | loop fusion | flops 3667968 | bytes 3164160 | tf_op jit(solution)/shard_map/reduce_sum | solution.py:149
  134.4 0.9 fusion.46
  135.3 1.4 collective-permute-start.3
  136.7 11.4 %psum.7 = f32[1,2048]{1,0:T(1,128)} all-reduce(f32[1,2048]{1,0:T(1,128)S(1)} %bitcast.80), channel_id=1, replica_groups=mesh['section'=8,'seq'=4] {'seq'}, use_global_device_ids=true, to_apply=%region_19.20 | all-reduce | flops 2048 | bytes 16384 | tf_op jit(solution)/shard_map/psum | solution.py:150
  148.1 0.8 copy.25
  (66 shorter events, 7.4 us)
Async XLA Ops:
  7.2 123.9 %reduce-scatter.2.cloned.1.call-start = ((), (), s32[]{:S(2)}) async-start(), calls=%async_computation.1 | async-start | bytes 2621440 | tf_op jit(solution)/shard_map/reduce_scatter | solution.py:128
  9.2 17.3 %collective-permute-start = (bf16[128,2048]{1,0:T(8,128)(2,1)}, bf16[128,2048]{1,0:T(8,128)(2,1)}, u32[]{:S(2)}, u32[]{:S(2)}) collective-permute-start(bf16[128,2048]{1,0:T(8,128)(2,1)} %fusion.34), channel_id=1, source_target_pairs={{0,1},{1,2},{2,3},{3,0},{4,5},{5,6},{6,7},{7,4},{8,9},{9,10},{10,1... | collective-permute-start | bytes 1572872 | tf_op jit(solution)/shard_map/ppermute | solution.py:21
  14.5 1.5 copy-start.4
  14.5 1.5 copy-start.6
  14.8 1.0 copy-start
  26.5 15.2 %collective-permute-start.1 = (bf16[128,2048]{1,0:T(8,128)(2,1)}, bf16[128,2048]{1,0:T(8,128)(2,1)}, u32[]{:S(2)}, u32[]{:S(2)}) collective-permute-start(bf16[128,2048]{1,0:T(8,128)(2,1)} %collective-permute-done), channel_id=1, source_target_pairs={{0,1},{1,2},{2,3},{3,0},{4,5},{5,6},{6,7},{7,4},{8,9},{9,10},{10,1... | collective-permute-start | bytes 1572872 | tf_op jit(solution)/shard_map/ppermute | solution.py:21
  41.7 14.3 %collective-permute-start.2 = (bf16[128,2048]{1,0:T(8,128)(2,1)}, bf16[128,2048]{1,0:T(8,128)(2,1)}, u32[]{:S(2)}, u32[]{:S(2)}) collective-permute-start(bf16[128,2048]{1,0:T(8,128)(2,1)} %collective-permute-done.1), channel_id=1, source_target_pairs={{0,1},{1,2},{2,3},{3,0},{4,5},{5,6},{6,7},{7,4},{8,9},{9,10},{10,1... | collective-permute-start | bytes 1572872 | tf_op jit(solution)/shard_map/ppermute | solution.py:21
  41.7 4.5 %copy-start.11 = (f32[1,2048]{1,0:T(1,128)S(1)}, f32[1,2048]{1,0:T(1,128)}, u32[]{:S(2)}) copy-start(f32[1,2048]{1,0:T(1,128)} %param.15) | copy-start | bytes 24580
  74.9 1.7 %copy-start.1 = (f32[512,512]{0,1:T(8,128)S(1)}, f32[512,512]{0,1:T(8,128)}, u32[]{:S(2)}) copy-start(f32[512,512]{0,1:T(8,128)} %copy-done) | copy-start | bytes 3145732
  74.9 1.7 %copy-start.9 = (bf16[512,512]{1,0:T(8,128)(2,1)S(1)}, bf16[512,512]{1,0:T(8,128)(2,1)}, u32[]{:S(2)}) copy-start(bf16[512,512]{1,0:T(8,128)(2,1)} %get-tuple-element.80) | copy-start | bytes 1572868
  74.9 1.9 %copy-start.10 = (bf16[512,512]{0,1:T(8,128)(2,1)S(1)}, bf16[512,512]{0,1:T(8,128)(2,1)}, u32[]{:S(2)}) copy-start(bf16[512,512]{0,1:T(8,128)(2,1)} %reduce_sum.140) | copy-start | bytes 1572868
  77.1 1.0 copy-start.7
  77.1 1.3 copy-start.5
  81.4 2.2 %slice-start = ((s8[6291456]{0:T(1024)(128)(4,1)}), s8[4194304]{0:T(1024)(128)(4,1)S(1)}, s32[]{:S(2)}) async-start(s8[6291456]{0:T(1024)(128)(4,1)} %bitcast.72), calls=%async_computation.2 | async-start | bytes 8388608
  81.7 2.6 %slice-start.1 = ((s8[6291456]{0:T(1024)(128)(4,1)}), s8[2097152]{0:T(1024)(128)(4,1)S(1)}, s32[]{:S(2)}) async-start(s8[6291456]{0:T(1024)(128)(4,1)} %bitcast.72), calls=%async_computation.3 | async-start | bytes 4194304
  89.5 1.0 copy-start.2
  89.5 1.5 copy-start.12
  89.5 1.5 copy-start.13
  89.5 43.0 %copy-start.3 = (bf16[1,128,2048]{2,1,0:T(8,128)(2,1)S(1)}, bf16[1,128,2048]{2,1,0:T(8,128)(2,1)}, u32[]{:S(2)}) copy-start(bf16[1,128,2048]{2,1,0:T(8,128)(2,1)} %param.9) | copy-start | bytes 1572868
  89.5 43.0 %copy-start.8 = (bf16[1,128,2048]{2,1,0:T(8,128)(2,1)S(1)}, bf16[1,128,2048]{2,1,0:T(8,128)(2,1)}, u32[]{:S(2)}) copy-start(bf16[1,128,2048]{2,1,0:T(8,128)(2,1)} %param.11) | copy-start | bytes 1572868
  135.3 12.8 %collective-permute-start.3 = (bf16[128,2048]{1,0:T(8,128)(2,1)S(1)}, bf16[128,2048]{1,0:T(8,128)(2,1)S(1)}, u32[]{:S(2)}, u32[]{:S(2)}) collective-permute-start(bf16[128,2048]{1,0:T(8,128)(2,1)S(1)} %get-tuple-element.83), channel_id=1, source_target_pairs={{0,4},{4,8},{8,12},{12,16},{16,20},{20,24},{24,28},{1,5},{5,9},{9,... | collective-permute-start | bytes 1572872 | tf_op jit(solution)/shard_map/ppermute | solution.py:30
Sparse Core Ops, SparseCore 0:
  89.7 41.3 reduce-scatter.1
